TPU v7x, 32 devices: a whole 2x2x4 slice. The times are simulated.
32 devices in a mesh: band: 8 (over z, y), head: 4 (over x, core).
Axes of the slice: x: 2, y: 2, z: 4, core: 2. Of those that a mesh axis runs over, the one named last changes fastest.
Arguments:
- grid_feat: bfloat16 [65536, 1024], P(('band', 'head')), may hold values from -7 to 7
- mesh_feat: bfloat16 [4096, 1024], P(('band', 'head')), may hold values from -7 to 7
- enc_query: bfloat16 [1024, 1024], replicated, may hold values from -0.1875 to 0.1875
- enc_keyval: bfloat16 [1024, 2048], replicated, may hold values from -0.1875 to 0.1875
- enc_out: bfloat16 [1024, 1024], replicated, may hold values from -0.1875 to 0.1875
- proc_qkv: bfloat16 [3, 1024, 1024], P(None, None, 'head'), may hold values from -0.1875 to 0.1875
- proc_out: bfloat16 [1024, 1024], P('head'), may hold values from -0.1875 to 0.1875
- tile_ids: int32 [64, 8], P(('band', 'head')), may hold values from 0 to 511, as said below
- key_counts: int32 [64], P(('band', 'head')), may hold values from 128 to 1024, as said below
Outputs:
- mesh_out: bfloat16 [4096, 1024], P(('band', 'head'))
Inputs may be any that keep to these rules, and one draw needn't show every extreme that they name: `tile_ids`: mesh tile m lies on the device that holds mesh rows m * 64; every tile it lists is one of that device's grid tiles (grid rows of the same device) or of the 2 grid tiles just before or just after them. Slots may repeat tiles. `key_counts`: the largest value is reached in every draw.
All inputs are finite; a program needn't handle non-finite values.
Results may differ from a plain program's by a relative error of at most 0.012.
The roundings to bfloat16 on the way count: a program that leaves them out, or rounds other values in their place, can miss the bound.
Values may be sent and summed in bfloat16 or wider, within the bound.
A program may use at most 128 MiB of HBM per device.

v0:
```python
import math
import jax
import jax.numpy as jnp
from jax import lax
from jax.sharding import PartitionSpec as P

D = 1024
HEADS = 16
HALFW = 512
GT = 128
LIST = 8
MT = 64
HALO_TILES = 2


def extended(shard, sides, width):
    for axis, dim in sides:
        size, length = (lax.axis_size(axis), shard.shape[dim])
        up = [(i, (i + 1) % size) for i in range(size - 1)]
        down = [(j, i) for i, j in up]
        last = lax.slice_in_dim(shard, length - width, length, axis=dim)
        first = lax.slice_in_dim(shard, 0, width, axis=dim)
        before = lax.ppermute(last, axis, up)
        after = lax.ppermute(first, axis, down)
        shard = jnp.concatenate([before, shard, after], axis=dim)
    return shard


def masked_softmax(scores, key_mask):
    scores = jnp.where(key_mask, scores, -1e30)
    row_top = jnp.max(scores, axis=-1, keepdims=True)
    weights = jnp.exp(scores - row_top)
    return (weights / jnp.sum(weights, axis=-1, keepdims=True)).astype(jnp.bfloat16)


def local(
    grid_feat, mesh_feat, enc_query, enc_keyval, enc_out, proc_qkv, proc_out, tile_ids, key_counts
):
    grid_count, model_width = grid_feat.shape
    mesh_count = mesh_feat.shape[0]
    tiles_dev = grid_count // GT
    head_size = D // HEADS
    score_scale = head_size ** (-0.5)
    device = lax.axis_index(("band", "head"))
    grid_kv = jnp.dot(grid_feat, enc_keyval, preferred_element_type=jnp.float32).astype(
        jnp.bfloat16
    )
    bordered = extended(
        grid_kv.reshape(tiles_dev, GT * 2 * model_width), ((("band", "head"), 0),), HALO_TILES
    )
    grid_tiles = bordered.reshape(-1, GT, 2 * model_width)
    queries = jnp.dot(mesh_feat, enc_query, preferred_element_type=jnp.float32).astype(jnp.bfloat16)
    local_lists = tile_ids - (device * tiles_dev - HALO_TILES)
    positions = jnp.arange(LIST * GT, dtype=jnp.int32)

    def one_tile(packed):
        query_tile, tile_list, valid = packed
        gathered = grid_tiles[tile_list].reshape(LIST * GT, 2 * model_width)
        key_rows = gathered[:, :model_width].reshape(LIST * GT, HEADS, head_size)
        value_rows = gathered[:, model_width:].reshape(LIST * GT, HEADS, head_size)
        query_heads = query_tile.reshape(MT, HEADS, head_size)
        scores = (
            jnp.einsum("qhd,khd->hqk", query_heads, key_rows, preferred_element_type=jnp.float32)
            * score_scale
        )
        weights = masked_softmax(scores, (positions < valid)[None, None, :])
        attended = jnp.einsum(
            "hqk,khd->qhd", weights, value_rows, preferred_element_type=jnp.float32
        )
        return attended.reshape(MT, model_width).astype(jnp.bfloat16)

    enc_attn = lax.map(
        one_tile, (queries.reshape(mesh_count // MT, MT, model_width), local_lists, key_counts)
    )
    enc_attn = enc_attn.reshape(mesh_count, model_width)
    mesh_state = (
        mesh_feat.astype(jnp.float32)
        + jnp.dot(enc_attn, enc_out, preferred_element_type=jnp.float32)
    ).astype(jnp.bfloat16)
    head_cols = proc_qkv.shape[2]
    piece = lax.all_gather(mesh_state, "head", axis=0, tiled=True)
    product = jnp.einsum("rd,tdc->rtc", piece, proc_qkv, preferred_element_type=jnp.float32)
    projected = product.astype(jnp.bfloat16).reshape(piece.shape[0], 3 * head_cols)
    group_rows = projected.shape[0]
    bordered_kv = extended(projected[:, head_cols:], (("band", 0),), HALFW)
    local_heads = head_cols // head_size
    block_rows = math.gcd(group_rows, 512)
    band_start = lax.axis_index("band") * group_rows
    mesh_total = group_rows * lax.axis_size("band")

    def one_block(block_index):
        first = block_index * block_rows
        span = block_rows + 2 * HALFW
        query_heads = lax.dynamic_slice_in_dim(projected, first, block_rows, 0)[
            :, :head_cols
        ].reshape(block_rows, local_heads, head_size)
        window_rows = lax.dynamic_slice_in_dim(bordered_kv, first, span, 0)
        key_rows = window_rows[:, :head_cols].reshape(span, local_heads, head_size)
        value_rows = window_rows[:, head_cols:].reshape(span, local_heads, head_size)
        query_pos = band_start + first + jnp.arange(block_rows, dtype=jnp.int32)
        key_pos = band_start + first - HALFW + jnp.arange(span, dtype=jnp.int32)
        near = (jnp.abs(query_pos[:, None] - key_pos[None, :]) < HALFW) & (
            (key_pos >= 0) & (key_pos < mesh_total)
        )[None, :]
        scores = (
            jnp.einsum("qhd,khd->hqk", query_heads, key_rows, preferred_element_type=jnp.float32)
            * score_scale
        )
        weights = masked_softmax(scores, near[None, :, :])
        attended = jnp.einsum(
            "hqk,khd->qhd", weights, value_rows, preferred_element_type=jnp.float32
        )
        return attended.reshape(block_rows, head_cols).astype(jnp.bfloat16)

    proc_attn = lax.map(one_block, jnp.arange(group_rows // block_rows, dtype=jnp.int32)).reshape(
        group_rows, head_cols
    )
    own_rows = lax.all_to_all(proc_attn, "head", split_axis=0, concat_axis=1, tiled=True)
    out_weights = lax.all_gather(proc_out, "head", axis=0, tiled=True)
    head_total = jnp.dot(own_rows, out_weights, preferred_element_type=jnp.float32)
    return (mesh_state.astype(jnp.float32) + head_total).astype(jnp.bfloat16)


def solution(mesh):
    return jax.shard_map(
        local,
        mesh=mesh,
        in_specs=(
            P(("band", "head"), None),
            P(("band", "head"), None),
            P(),
            P(),
            P(),
            P(None, None, "head"),
            P("head", None),
            P(("band", "head"), None),
            P(("band", "head")),
        ),
        out_specs=P(("band", "head"), None),
        check_vma=False,
    )
```

profile of v0, /device:TPU:8, one launch (start us, length us, event | category | flops | bytes accessed | tf_op | source)
XLA Modules:
  0.0 208.6 jit_solution(7345442903268691120)
XLA Ops:
  6.5 0.0 copy-start
  6.5 0.0 all-gather.3.cloned.1.call-start
  6.5 12.1 %convolution_convert_fusion = bf16[2048,2048]{1,0:T(8,128)(2,1)S(1)} fusion(bf16[2048,1024]{1,0:T(8,128)(2,1)} %param.11, bf16[1024,2048]{1,0:T(8,128)(2,1)} %param.14), kind=kOutput, calls=%fused_computation.30 | convolution fusion | flops 8594128896 | bytes 16777216 | tf_op jit(solution)/shard_map/dot_general | solution.py:45
  18.6 0.0 copy-start.3
  18.6 3.3 %copy-done.3 = bf16[2048,2048]{1,0:T(8,128)(2,1)} copy-done((bf16[2048,2048]{1,0:T(8,128)(2,1)}, bf16[2048,2048]{1,0:T(8,128)(2,1)S(1)}, u32[]{:S(2)}) %copy-start.3) | copy-done | bytes 8388632
  21.9 1.2 fusion.33
  23.1 3.0 %slice.36 = bf16[2,262144]{1,0:T(2,128)(2,1)} reshape(bf16[256,2048]{1,0:T(8,128)(2,1)} %get-tuple-element.89) | data formatting | bytes 2097152 | tf_op jit(solution)/shard_map/slice | solution.py:22
  26.1 3.7 %collective-permute-start.1 = (bf16[2,262144]{1,0:T(2,128)(2,1)}, bf16[2,262144]{1,0:T(2,128)(2,1)}, u32[]{:S(2)}, u32[]{:S(2)}) collective-permute-start(bf16[2,262144]{1,0:T(2,128)(2,1)} %slice.36), channel_id=1, source_target_pairs={{1,0},{2,1},{3,2},{4,3},{5,4},{6,5},{7,6},{8,7},{9,8},{10,9},{11,1... | collective-permute-start | bytes 3145736 | tf_op jit(solution)/shard_map/ppermute | solution.py:24
  29.8 1.7 slice.34
  31.5 2.1 %collective-permute-start = (bf16[2,262144]{1,0:T(2,128)(2,1)}, bf16[2,262144]{1,0:T(2,128)(2,1)}, u32[]{:S(2)}, u32[]{:S(2)}) collective-permute-start(bf16[2,262144]{1,0:T(2,128)(2,1)} %slice.34), channel_id=1, source_target_pairs={{0,1},{1,2},{2,3},{3,4},{4,5},{5,6},{6,7},{7,8},{8,9},{9,10},{10,1... | collective-permute-start | bytes 3145736 | tf_op jit(solution)/shard_map/ppermute | solution.py:23
  33.6 0.0 copy-done.6
  33.7 0.0 copy-done
  33.7 0.0 copy-done.5
  33.7 0.4 convolution_convert_fusion.2
  34.1 8.3 %collective-permute-done.1 = bf16[2,262144]{1,0:T(2,128)(2,1)} collective-permute-done((bf16[2,262144]{1,0:T(2,128)(2,1)}, bf16[2,262144]{1,0:T(2,128)(2,1)}, u32[]{:S(2)}, u32[]{:S(2)}) %collective-permute-start.1) | collective-permute-done | bytes 1048608 | tf_op jit(solution)/shard_map/ppermute | solution.py:24
  42.4 1.6 copy.30
  44.0 5.8 %collective-permute-done = bf16[2,262144]{1,0:T(2,128)(2,1)} collective-permute-done((bf16[2,262144]{1,0:T(2,128)(2,1)}, bf16[2,262144]{1,0:T(2,128)(2,1)}, u32[]{:S(2)}, u32[]{:S(2)}) %collective-permute-start) | collective-permute-done | bytes 1048608 | tf_op jit(solution)/shard_map/ppermute | solution.py:23
  49.8 1.6 copy.31
  51.4 0.0 copy-start.7
  51.4 10.7 %pad_maximum_fusion = bf16[20,128,2048]{2,1,0:T(8,128)(2,1)} fusion(bf16[2,128,2048]{2,1,0:T(8,128)(2,1)S(1)} %bitcast.79, bf16[16,128,2048]{2,1,0:T(8,128)(2,1)} %bitcast.77, bf16[2,128,2048]{2,1,0:T(8,128)(2,1)S(1)} %bitcast.80), kind=kLoop, calls=%fused_computation.28 | loop fusion | flops 10485760 | bytes 20971520 | tf_op jit(solution)/shard_map/concatenate | solution.py:25
  62.1 52.4 %while.3 = (s32[]{:T(128)}, bf16[2,64,1024]{2,1,0:T(8,128)(2,1)S(1)}, s32[2,8]{1,0:T(2,128)S(1)}, bf16[20,128,2048]{2,1,0:T(8,128)(2,1)}, s32[2]{0:T(128)S(1)}, /*index=5*/bf16[2,64,1024]{2,1,0:T(8,128)(2,1)S(1)}, s32[]{:T(128)}) while((s32[]{:T(128)}, bf16[2,64,1024]{2,1,0:T(8,128)(2,1)S(1)}, s32[2,8]{1,0:T(2,128)S(1)}, ...), condition=%wide.region_3.4_spmd.clone, body=%wide.region_0.3_spmd.clone.sunk | while | flops 276892704 | bytes 55851268 | solution.py:72
  62.2 6.8 %gather_fusion = bf16[8,128,2048]{2,1,0:T(8,128)(2,1)} fusion(bf16[20,128,2048]{2,1,0:T(8,128)(2,1)} %get-tuple-element.156, s32[1024]{0:T(1024)S(1)} %pad_clamp_fusion.2), kind=kCustom, calls=%fused_computation.clone.clone.1 | custom fusion | bytes 8388640 | tf_op jit(solution)/shard_map/while/body/eval_jaxpr/gather | solution.py:58
  69.0 4.6 %fusion.64 = (bf16[1024,1024]{1,0:T(8,128)(2,1)}, bf16[1024,1024]{1,0:T(8,128)(2,1)}) fusion(bf16[1024,2048]{1,0:T(8,128)(2,1)} %bitcast.74), kind=kLoop, calls=%fused_computation.56.clone.1 | loop fusion | bytes 8388608 | tf_op jit(solution)/shard_map/while/body/eval_jaxpr/slice | solution.py:59
  73.6 2.9 %copy.38 = bf16[1024,1024]{0,1:T(8,128)(2,1)S(1)} copy(bf16[1024,1024]{1,0:T(8,128)(2,1)} %get-tuple-element.136) | data formatting | bytes 4194304 | tf_op jit(solution)/shard_map/while
  76.5 0.2 reshape.183
  76.7 0.7 fusion.65
  77.4 0.6 dynamic_slice.35
  78.0 0.6 iota_compare_fusion.2
  78.7 3.3 %fusion.66 = (f32[16,64]{1,0:T(8,128)S(1)}, f32[16,64,1024]{2,1,0:T(8,128)}) fusion(f32[16,64,1024]{2,1,0:T(8,128)S(1)} %fusion.65, pred[1024]{0:T(1024)(128)(4,1)S(1)} %iota_compare_fusion.2), kind=kOutput, calls=%fused_computation.57.clone.1 | output fusion | flops 6292479 | bytes 8393728 | tf_op jit(solution)/shard_map/while/body/eval_jaxpr/sub | solution.py:32
  82.0 2.6 %copy.37 = bf16[1024,1024]{0,1:T(8,128)(2,1)} copy(bf16[1024,1024]{1,0:T(8,128)(2,1)S(1)} %copy-done.2) | data formatting | bytes 4194304 | tf_op jit(solution)/shard_map/while
  84.6 3.6 %fusion.67 = bf16[16,64,64]{2,1,0:T(8,128)(2,1)S(1)} fusion(bf16[1024,16,64]{0,2,1:T(8,128)(2,1)} %bitcast.76, f32[16,64,1024]{2,1,0:T(8,128)} %get-tuple-element.137, f32[16,64]{1,0:T(8,128)S(1)} %get-tuple-element.138), kind=kOutput, calls=%fused_computation.11.clone.1 | convolution fusion | flops 136380416 | bytes 6426624 | tf_op jit(solution)/shard_map/while/body/eval_jaxpr/hqk,khd->qhd/dot_general | solution.py:67
  88.2 0.1 copy.39
  88.4 6.8 %gather_fusion = bf16[8,128,2048]{2,1,0:T(8,128)(2,1)} fusion(bf16[20,128,2048]{2,1,0:T(8,128)(2,1)} %get-tuple-element.156, s32[1024]{0:T(1024)S(1)} %pad_clamp_fusion.2), kind=kCustom, calls=%fused_computation.clone.clone.1 | custom fusion | bytes 8388640 | tf_op jit(solution)/shard_map/while/body/eval_jaxpr/gather | solution.py:58
  95.2 4.6 %fusion.64 = (bf16[1024,1024]{1,0:T(8,128)(2,1)}, bf16[1024,1024]{1,0:T(8,128)(2,1)}) fusion(bf16[1024,2048]{1,0:T(8,128)(2,1)} %bitcast.74), kind=kLoop, calls=%fused_computation.56.clone.1 | loop fusion | bytes 8388608 | tf_op jit(solution)/shard_map/while/body/eval_jaxpr/slice | solution.py:59
  99.8 2.9 %copy.38 = bf16[1024,1024]{0,1:T(8,128)(2,1)S(1)} copy(bf16[1024,1024]{1,0:T(8,128)(2,1)} %get-tuple-element.136) | data formatting | bytes 4194304 | tf_op jit(solution)/shard_map/while
  102.7 0.2 reshape.183
  102.9 0.7 fusion.65
  103.6 0.6 dynamic_slice.35
  104.2 0.6 iota_compare_fusion.2
  104.9 3.3 %fusion.66 = (f32[16,64]{1,0:T(8,128)S(1)}, f32[16,64,1024]{2,1,0:T(8,128)}) fusion(f32[16,64,1024]{2,1,0:T(8,128)S(1)} %fusion.65, pred[1024]{0:T(1024)(128)(4,1)S(1)} %iota_compare_fusion.2), kind=kOutput, calls=%fused_computation.57.clone.1 | output fusion | flops 6292479 | bytes 8393728 | tf_op jit(solution)/shard_map/while/body/eval_jaxpr/sub | solution.py:32
  108.2 2.6 %copy.37 = bf16[1024,1024]{0,1:T(8,128)(2,1)} copy(bf16[1024,1024]{1,0:T(8,128)(2,1)S(1)} %copy-done.2) | data formatting | bytes 4194304 | tf_op jit(solution)/shard_map/while
  110.8 3.6 %fusion.67 = bf16[16,64,64]{2,1,0:T(8,128)(2,1)S(1)} fusion(bf16[1024,16,64]{0,2,1:T(8,128)(2,1)} %bitcast.76, f32[16,64,1024]{2,1,0:T(8,128)} %get-tuple-element.137, f32[16,64]{1,0:T(8,128)S(1)} %get-tuple-element.138), kind=kOutput, calls=%fused_computation.11.clone.1 | convolution fusion | flops 136380416 | bytes 6426624 | tf_op jit(solution)/shard_map/while/body/eval_jaxpr/hqk,khd->qhd/dot_general | solution.py:67
  114.4 0.1 copy.39
  114.5 2.7 %fusion.23 = bf16[128,1024]{1,0:T(8,128)(2,1)} fusion(bf16[128,1024]{1,0:T(8,128)(2,1)S(1)} %bitcast.88, bf16[1024,1024]{1,0:T(8,128)(2,1)} %param.15, bf16[128,1024]{1,0:T(8,128)(2,1)S(1)} %copy-done.5), kind=kOutput, calls=%fused_computation.43 | convolution fusion | flops 268828672 | bytes 2883584 | tf_op jit(solution)/shard_map/dot_general | solution.py:78
  117.3 0.0 all-gather.3.cloned.1.call-update
  117.3 0.0 all-gather.5.cloned.1.call-start
  117.4 0.7 all-gather.5.cloned.1.call-update
  118.1 21.6 %all-gather.3.cloned.1.call-done = bf16[512,1024]{1,0:T(8,128)(2,1)} async-done(((bf16[128,1024]{1,0:T(8,128)(2,1)}), bf16[512,1024]{1,0:T(8,128)(2,1)}) %all-gather.3.cloned.1.call-update) | async-done | bytes 1048592 | tf_op jit(solution)/shard_map/all_gather | solution.py:81
  139.7 2.8 %convolution_convert_fusion.1 = bf16[512,3,256]{0,2,1:T(8,128)(2,1)S(1)} fusion(bf16[3,1024,256]{2,1,0:T(8,128)(2,1)} %param.16, bf16[512,1024]{1,0:T(8,128)(2,1)} %all-gather.3.cloned.1.call-done), kind=kOutput, calls=%fused_computation.38 | convolution fusion | flops 805699584 | bytes 3407872 | tf_op jit(solution)/shard_map/rd,tdc->rtc/dot_general | solution.py:82
  142.5 3.4 %collective-permute-start.2 = (bf16[512,512]{0,1:T(8,128)(2,1)S(1)}, bf16[512,512]{0,1:T(8,128)(2,1)S(1)}, u32[]{:S(2)}, u32[]{:S(2)}) collective-permute-start(bf16[512,512]{0,1:T(8,128)(2,1)S(1)} %slice.49), channel_id=1, source_target_pairs={{0,4},{4,8},{8,12},{12,16},{16,20},{20,24},{24,28},{1,5},{5,9},{9,... | collective-permute-start | bytes 1572872 | tf_op jit(solution)/shard_map/ppermute | solution.py:23
  145.9 3.6 %collective-permute-start.3 = (bf16[512,512]{0,1:T(8,128)(2,1)S(1)}, bf16[512,512]{0,1:T(8,128)(2,1)S(1)}, u32[]{:S(2)}, u32[]{:S(2)}) collective-permute-start(bf16[512,512]{0,1:T(8,128)(2,1)S(1)} %slice.49), channel_id=1, source_target_pairs={{4,0},{8,4},{12,8},{16,12},{20,16},{24,20},{28,24},{5,1},{9,5},{13... | collective-permute-start | bytes 1572872 | tf_op jit(solution)/shard_map/ppermute | solution.py:24
  149.5 1.0 fusion.21
  150.5 18.2 %collective-permute-done.2 = bf16[512,512]{0,1:T(8,128)(2,1)S(1)} collective-permute-done((bf16[512,512]{0,1:T(8,128)(2,1)S(1)}, bf16[512,512]{0,1:T(8,128)(2,1)S(1)}, u32[]{:S(2)}, u32[]{:S(2)}) %collective-permute-start.2) | collective-permute-done | bytes 524320 | tf_op jit(solution)/shard_map/ppermute | solution.py:23
  168.6 1.9 collective-permute-done.3
  170.5 0.1 pad_maximum_fusion.1
  170.6 1.3 fusion.34
  171.9 9.8 %fusion.35 = (f32[4,512]{1,0:T(4,128)S(1)}, f32[4,512,1536]{2,1,0:T(8,128)}) fusion(pred[512,1536]{1,0:T(8,128)(4,1)S(1)} %fusion.21, bf16[512,4,64]{0,2,1:T(8,128)(2,1)S(1)} %bitcast.87, bf16[1536,4,64]{0,2,1:T(8,128)(2,1)} %bitcast.86), kind=kOutput, calls=%fused_computation.60 | convolution fusion | flops 415237632 | bytes 14426112 | tf_op jit(solution)/shard_map/while/body/eval_jaxpr/sub | solution.py:32
  181.7 7.0 %fusion.25 = bf16[512,4,64]{0,2,1:T(8,128)(2,1)S(1)} fusion(bf16[1536,4,64]{0,2,1:T(8,128)(2,1)} %bitcast.85, f32[4,512,1536]{2,1,0:T(8,128)} %get-tuple-element.93, f32[4,512]{1,0:T(4,128)S(1)} %get-tuple-element.92), kind=kOutput, calls=%fused_computation.45 | convolution fusion | flops 409075712 | bytes 13639680 | tf_op jit(solution)/shard_map/while/body/eval_jaxpr/hqk,khd->qhd/dot_general | solution.py:110
  188.8 0.1 convert_element_type.65
  188.9 0.7 copy.18
  189.6 3.4 %all-to-all-start = ((bf16[4,128,256]{1,2,0:T(8,128)(2,1)}), bf16[4,128,256]{1,2,0:T(8,128)(2,1)S(1)}, u32[]{:S(2)}, u32[]{:S(2)}) async-start(bf16[4,128,256]{1,2,0:T(8,128)(2,1)} %copy.18), calls=%async_computation | async-start | bytes 524288 | tf_op jit(solution)/shard_map/all_to_all | solution.py:118
  193.0 0.0 all-gather.5.cloned.1.call-done
  193.0 5.9 %all-to-all-done = bf16[4,128,256]{1,2,0:T(8,128)(2,1)S(1)} async-done(((bf16[4,128,256]{1,2,0:T(8,128)(2,1)}), bf16[4,128,256]{1,2,0:T(8,128)(2,1)S(1)}, u32[]{:S(2)}, u32[]{:S(2)}) %all-to-all-start) | async-done | bytes 262176 | tf_op jit(solution)/shard_map/all_to_all | solution.py:118
  199.0 2.8 %fusion.24 = bf16[128,1024]{1,0:T(8,128)(2,1)} fusion(bf16[128,1024]{0,1:T(8,128)(2,1)S(1)} %bitcast.82, bf16[1024,1024]{1,0:T(8,128)(2,1)} %all-gather.5.cloned.1.call-done, bf16[128,1024]{1,0:T(8,128)(2,1)S(1)} %copy-done.4), kind=kOutput, calls=%fused_computation.44 | convolution fusion | flops 268828672 | bytes 2883584 | tf_op jit(solution)/shard_map/dot_general | solution.py:120
  (26 shorter events, 0.2 us)
Async XLA Ops:
  6.5 27.1 %copy-start = (bf16[1024,1024]{1,0:T(8,128)(2,1)S(1)}, bf16[1024,1024]{1,0:T(8,128)(2,1)}, u32[]{:S(2)}) copy-start(bf16[1024,1024]{1,0:T(8,128)(2,1)} %param.13) | copy-start | bytes 6291460
  6.5 133.1 %all-gather.3.cloned.1.call-start = ((), (), s32[]{:S(2)}) async-start(), calls=%async_computation.1 | async-start | bytes 1310720 | tf_op jit(solution)/shard_map/all_gather | solution.py:81
  18.6 3.3 %copy-start.3 = (bf16[2048,2048]{1,0:T(8,128)(2,1)}, bf16[2048,2048]{1,0:T(8,128)(2,1)S(1)}, u32[]{:S(2)}) copy-start(bf16[2048,2048]{1,0:T(8,128)(2,1)S(1)} %convolution_convert_fusion) | copy-start | bytes 25165828
  21.9 11.7 %copy-start.6 = (s32[2,8]{1,0:T(2,128)S(1)}, s32[2,8]{1,0:T(2,128)}, u32[]{:S(2)}) copy-start(s32[2,8]{1,0:T(2,128)} %param.18) | copy-start | bytes 196
  21.9 11.7 %copy-start.5 = (bf16[128,1024]{1,0:T(8,128)(2,1)S(1)}, bf16[128,1024]{1,0:T(8,128)(2,1)}, u32[]{:S(2)}) copy-start(bf16[128,1024]{1,0:T(8,128)(2,1)} %param.12) | copy-start | bytes 786436
  26.1 16.3 %collective-permute-start.1 = (bf16[2,262144]{1,0:T(2,128)(2,1)}, bf16[2,262144]{1,0:T(2,128)(2,1)}, u32[]{:S(2)}, u32[]{:S(2)}) collective-permute-start(bf16[2,262144]{1,0:T(2,128)(2,1)} %slice.36), channel_id=1, source_target_pairs={{1,0},{2,1},{3,2},{4,3},{5,4},{6,5},{7,6},{8,7},{9,8},{10,9},{11,1... | collective-permute-start | bytes 3145736 | tf_op jit(solution)/shard_map/ppermute | solution.py:24
  31.5 18.3 %collective-permute-start = (bf16[2,262144]{1,0:T(2,128)(2,1)}, bf16[2,262144]{1,0:T(2,128)(2,1)}, u32[]{:S(2)}, u32[]{:S(2)}) collective-permute-start(bf16[2,262144]{1,0:T(2,128)(2,1)} %slice.34), channel_id=1, source_target_pairs={{0,1},{1,2},{2,3},{3,4},{4,5},{5,6},{6,7},{7,8},{8,9},{9,10},{10,1... | collective-permute-start | bytes 3145736 | tf_op jit(solution)/shard_map/ppermute | solution.py:23
  51.4 10.7 %copy-start.7 = (s32[2]{0:T(128)S(1)}, s32[2]{0:T(128)}, u32[]{:S(2)}) copy-start(s32[2]{0:T(128)} %param.19) | copy-start | bytes 28
  78.6 3.3 %copy-start.2 = (bf16[1024,1024]{1,0:T(8,128)(2,1)S(1)}, bf16[1024,1024]{1,0:T(8,128)(2,1)}, u32[]{:S(2)}) copy-start(bf16[1024,1024]{1,0:T(8,128)(2,1)} %get-tuple-element.135) | copy-start | bytes 6291460 | tf_op jit(solution)/shard_map/while
  104.9 3.3 %copy-start.2 = (bf16[1024,1024]{1,0:T(8,128)(2,1)S(1)}, bf16[1024,1024]{1,0:T(8,128)(2,1)}, u32[]{:S(2)}) copy-start(bf16[1024,1024]{1,0:T(8,128)(2,1)} %get-tuple-element.135) | copy-start | bytes 6291460 | tf_op jit(solution)/shard_map/while
  117.3 75.7 %all-gather.5.cloned.1.call-start = ((), (), s32[]{:S(2)}) async-start(), calls=%async_computation.2 | async-start | bytes 2621440 | tf_op jit(solution)/shard_map/all_gather | solution.py:119
  142.5 26.2 %collective-permute-start.2 = (bf16[512,512]{0,1:T(8,128)(2,1)S(1)}, bf16[512,512]{0,1:T(8,128)(2,1)S(1)}, u32[]{:S(2)}, u32[]{:S(2)}) collective-permute-start(bf16[512,512]{0,1:T(8,128)(2,1)S(1)} %slice.49), channel_id=1, source_target_pairs={{0,4},{4,8},{8,12},{12,16},{16,20},{20,24},{24,28},{1,5},{5,9},{9,... | collective-permute-start | bytes 1572872 | tf_op jit(solution)/shard_map/ppermute | solution.py:23
  145.9 24.7 %collective-permute-start.3 = (bf16[512,512]{0,1:T(8,128)(2,1)S(1)}, bf16[512,512]{0,1:T(8,128)(2,1)S(1)}, u32[]{:S(2)}, u32[]{:S(2)}) collective-permute-start(bf16[512,512]{0,1:T(8,128)(2,1)S(1)} %slice.49), channel_id=1, source_target_pairs={{4,0},{8,4},{12,8},{16,12},{20,16},{24,20},{28,24},{5,1},{9,5},{13... | collective-permute-start | bytes 1572872 | tf_op jit(solution)/shard_map/ppermute | solution.py:24
  181.7 17.3 %copy-start.4 = (bf16[128,1024]{1,0:T(8,128)(2,1)S(1)}, bf16[128,1024]{1,0:T(8,128)(2,1)}, u32[]{:S(2)}) copy-start(bf16[128,1024]{1,0:T(8,128)(2,1)} %fusion.23) | copy-start | bytes 786436
  181.7 20.0 %copy-start.1 = (bf16[1024,1024]{1,0:T(8,128)(2,1)S(1)}, bf16[1024,1024]{1,0:T(8,128)(2,1)}, u32[]{:S(2)}) copy-start(bf16[1024,1024]{1,0:T(8,128)(2,1)} %param.13) | copy-start | bytes 6291460
  189.6 9.4 %all-to-all-start = ((bf16[4,128,256]{1,2,0:T(8,128)(2,1)}), bf16[4,128,256]{1,2,0:T(8,128)(2,1)S(1)}, u32[]{:S(2)}, u32[]{:S(2)}) async-start(bf16[4,128,256]{1,2,0:T(8,128)(2,1)} %copy.18), calls=%async_computation | async-start | bytes 524288 | tf_op jit(solution)/shard_map/all_to_all | solution.py:118
Sparse Core Ops, SparseCore 0:
  117.4 22.1 all-gather.2
  141.2 22.5 all-gather.4
where the time goes:
time: 209 us
  waiting for transfers between devices  62.4 us (30%)
  local copies, waits for them, and re-layouts  50.2 us (24%)
  matrix products  46.2 us (22%)
  other arithmetic  19.7 us (9%)
  starting transfers between devices  16.2 us (8%)
  between operations  13.6 us (7%)
    ppermute x2, waiting for transfers between devices, extended(): before = lax.ppermute(last, axis, up)  24 us
    all_gather x1, waiting for transfers between devices, local(): piece = lax.all_gather(mesh_state, 'head', axis=0, tiled=True)  21.6 us
    gather x2, local copies, waits for them, and re-layouts, one_tile(): gathered = grid_tiles[tile_list].reshape(LIST * GT, 2 * model_width)  13.7 us
    dot_general x1, matrix products, local(): jnp.dot(grid_feat, enc_keyval, preferred_element_type=jnp.float32)  12.1 us
    while x8, local copies, waits for them, and re-layouts  10.9 us
    concatenate x2, other arithmetic, extended(): shard = jnp.concatenate([before, shard, after], axis=dim)  10.8 us
    ppermute x2, waiting for transfers between devices, extended(): after = lax.ppermute(first, axis, down)  10.2 us
    sub x1, matrix products, masked_softmax(): weights = jnp.exp(scores - row_top)  9.82 us
  transfers between devices with their start and end apart: 7, of which 6 were waited for; matrix products, arithmetic and copies ran while one was open for 13% of the time, Pallas kernels for 0%

commit v1 on v0

--- a/solution.py
+++ b/solution.py
@@ -78,7 +78,14 @@
         + jnp.dot(enc_attn, enc_out, preferred_element_type=jnp.float32)
     ).astype(jnp.bfloat16)
     head_cols = proc_qkv.shape[2]
-    piece = lax.all_gather(mesh_state, "head", axis=0, tiled=True)
+    peers = lax.axis_size("head")
+    right = [(i_2, (i_2 + 1) % peers) for i_2 in range(peers)]
+    parts = [mesh_state]
+    for stride in range(1, peers):
+        parts = [lax.ppermute(parts[0], "head", right), *parts]
+    full = jnp.concatenate(parts, axis=0)
+    offset = (lax.axis_index("head") + 1) * parts[-1].shape[0]
+    piece = jnp.roll(full, offset, axis=0)
     product = jnp.einsum("rd,tdc->rtc", piece, proc_qkv, preferred_element_type=jnp.float32)
     projected = product.astype(jnp.bfloat16).reshape(piece.shape[0], 3 * head_cols)
     group_rows = projected.shape[0]

time: 209 us -> 205 us (0.981)
  waiting for transfers between devices: 62.4 us -> 43.1 us
  blocking collectives: 0 us -> 8.39 us
  starting transfers between devices: 16.2 us -> 24.4 us
    all_gather x1 -> x0, waiting for transfers between devices: 21.6 us -> none  [local(): piece = lax.all_gather(mesh_state, 'head', axis=0, tiled=True)]
    ppermute x0 -> x3, starting transfers between devices: none -> 11 us  [local(): parts = [lax.ppermute(parts[0], 'head', right), *parts]]
    all_to_all x0 -> x1, blocking collectives: none -> 8.39 us  [local(): lax.all_to_all(proc_attn, 'head', split_axis=0, concat_axis=1, tiled=True)]
    ppermute x0 -> x3, waiting for transfers between devices: none -> 8.21 us  [local(): parts = [lax.ppermute(parts[0], 'head', right), *parts]]
    all_to_all x1 -> x0, waiting for transfers between devices: 5.94 us -> none  [local(): lax.all_to_all(proc_attn, 'head', split_axis=0, concat_axis=1, tiled=True)]
    all_to_all x1 -> x0, starting transfers between devices: 3.4 us -> none  [local(): lax.all_to_all(proc_attn, 'head', split_axis=0, concat_axis=1, tiled=True)]
    unnamed x16 -> x21, local copies, waits for them, and re-layouts: 6.48 us -> 6.62 us
  transfers between devices with their start and end apart: 7 -> 8, of which waited for: 6 -> 7; matrix products, arithmetic and copies ran while one was open for 13% -> 13% of each run, Pallas kernels for 0% -> 0%
where the time goes in v1:
time: 205 us; the launch traced here: 204 us
  local copies, waits for them, and re-layouts  49.7 us (24%)
  matrix products  45.2 us (22%)
  waiting for transfers between devices  43.1 us (21%)
  starting transfers between devices  24.4 us (12%)
  other arithmetic  19.5 us (10%)
  between operations  13.7 us (7%)
  blocking collectives  8.39 us (4%)
    ppermute x2, waiting for transfers between devices, extended(): before = lax.ppermute(last, axis, up)  25.1 us
    gather x2, local copies, waits for them, and re-layouts, one_tile(): gathered = grid_tiles[tile_list].reshape(LIST * GT, 2 * model_width)  13.7 us
    dot_general x1, matrix products, local(): jnp.dot(grid_feat, enc_keyval, preferred_element_type=jnp.float32)  12.1 us
    ppermute x3, starting transfers between devices, local(): parts = [lax.ppermute(parts[0], 'head', right), *parts]  11 us
    while x8, local copies, waits for them, and re-layouts  10.8 us
    concatenate x2, other arithmetic, extended(): shard = jnp.concatenate([before, shard, after], axis=dim)  10.8 us
    sub x1, matrix products, masked_softmax(): weights = jnp.exp(scores - row_top)  9.82 us
    ppermute x2, waiting for transfers between devices, extended(): after = lax.ppermute(first, axis, down)  9.75 us
  transfers between devices with their start and end apart: 8, of which 7 were waited for; matrix products, arithmetic and copies ran while one was open for 13% of the time, Pallas kernels for 0%

profile of v1, /device:TPU:8, one launch (start us, length us, event | category | flops | bytes accessed | tf_op | source)
XLA Modules:
  0.0 204.1 jit_solution(6309490997285459647)
XLA Ops:
  6.5 0.0 copy-start
  6.5 0.0 all-gather.2.cloned.1.call-start
  6.5 12.1 %convolution_convert_fusion = bf16[2048,2048]{1,0:T(8,128)(2,1)S(1)} fusion(bf16[2048,1024]{1,0:T(8,128)(2,1)} %param.11, bf16[1024,2048]{1,0:T(8,128)(2,1)} %param.14), kind=kOutput, calls=%fused_computation.30 | convolution fusion | flops 8594128896 | bytes 16777216 | tf_op jit(solution)/shard_map/dot_general | solution.py:45
  18.6 0.0 copy-start.3
  18.6 3.3 %copy-done.3 = bf16[2048,2048]{1,0:T(8,128)(2,1)} copy-done((bf16[2048,2048]{1,0:T(8,128)(2,1)}, bf16[2048,2048]{1,0:T(8,128)(2,1)S(1)}, u32[]{:S(2)}) %copy-start.3) | copy-done | bytes 8388632
  21.9 1.2 fusion.35
  23.1 3.0 %slice.36 = bf16[2,262144]{1,0:T(2,128)(2,1)} reshape(bf16[256,2048]{1,0:T(8,128)(2,1)} %get-tuple-element.89) | data formatting | bytes 2097152 | tf_op jit(solution)/shard_map/slice | solution.py:22
  26.2 3.7 %collective-permute-start.1 = (bf16[2,262144]{1,0:T(2,128)(2,1)}, bf16[2,262144]{1,0:T(2,128)(2,1)}, u32[]{:S(2)}, u32[]{:S(2)}) collective-permute-start(bf16[2,262144]{1,0:T(2,128)(2,1)} %slice.36), channel_id=1, source_target_pairs={{1,0},{2,1},{3,2},{4,3},{5,4},{6,5},{7,6},{8,7},{9,8},{10,9},{11,1... | collective-permute-start | bytes 3145736 | tf_op jit(solution)/shard_map/ppermute | solution.py:24
  29.8 1.8 slice.34
  31.6 2.1 %collective-permute-start = (bf16[2,262144]{1,0:T(2,128)(2,1)}, bf16[2,262144]{1,0:T(2,128)(2,1)}, u32[]{:S(2)}, u32[]{:S(2)}) collective-permute-start(bf16[2,262144]{1,0:T(2,128)(2,1)} %slice.34), channel_id=1, source_target_pairs={{0,1},{1,2},{2,3},{3,4},{4,5},{5,6},{6,7},{7,8},{8,9},{9,10},{10,1... | collective-permute-start | bytes 3145736 | tf_op jit(solution)/shard_map/ppermute | solution.py:23
  33.7 0.0 copy-done.5
  33.8 0.4 convolution_convert_fusion.2
  34.2 8.3 %collective-permute-done.1 = bf16[2,262144]{1,0:T(2,128)(2,1)} collective-permute-done((bf16[2,262144]{1,0:T(2,128)(2,1)}, bf16[2,262144]{1,0:T(2,128)(2,1)}, u32[]{:S(2)}, u32[]{:S(2)}) %collective-permute-start.1) | collective-permute-done | bytes 1048608 | tf_op jit(solution)/shard_map/ppermute | solution.py:24
  42.5 1.6 copy.30
  44.1 5.8 %collective-permute-done = bf16[2,262144]{1,0:T(2,128)(2,1)} collective-permute-done((bf16[2,262144]{1,0:T(2,128)(2,1)}, bf16[2,262144]{1,0:T(2,128)(2,1)}, u32[]{:S(2)}, u32[]{:S(2)}) %collective-permute-start) | collective-permute-done | bytes 1048608 | tf_op jit(solution)/shard_map/ppermute | solution.py:23
  49.9 1.6 copy.31
  51.5 0.0 copy-start.6
  51.5 10.7 %pad_maximum_fusion = bf16[20,128,2048]{2,1,0:T(8,128)(2,1)} fusion(bf16[2,128,2048]{2,1,0:T(8,128)(2,1)S(1)} %bitcast.79, bf16[16,128,2048]{2,1,0:T(8,128)(2,1)} %bitcast.77, bf16[2,128,2048]{2,1,0:T(8,128)(2,1)S(1)} %bitcast.80), kind=kLoop, calls=%fused_computation.28 | loop fusion | flops 10485760 | bytes 20971520 | tf_op jit(solution)/shard_map/concatenate | solution.py:25
  62.2 52.1 %while.3 = (s32[]{:T(128)}, bf16[2,64,1024]{2,1,0:T(8,128)(2,1)S(1)}, s32[2,8]{1,0:T(2,128)S(1)}, bf16[20,128,2048]{2,1,0:T(8,128)(2,1)}, s32[2]{0:T(128)S(1)}, /*index=5*/bf16[2,64,1024]{2,1,0:T(8,128)(2,1)S(1)}, s32[]{:T(128)}) while((s32[]{:T(128)}, bf16[2,64,1024]{2,1,0:T(8,128)(2,1)S(1)}, s32[2,8]{1,0:T(2,128)S(1)}, ...), condition=%wide.region_3.4_spmd.clone, body=%wide.region_0.3_spmd.clone.sunk | while | flops 276892704 | bytes 55851268 | solution.py:72
  62.2 6.8 %gather_fusion = bf16[8,128,2048]{2,1,0:T(8,128)(2,1)} fusion(bf16[20,128,2048]{2,1,0:T(8,128)(2,1)} %get-tuple-element.156, s32[1024]{0:T(1024)S(1)} %pad_clamp_fusion.2), kind=kCustom, calls=%fused_computation.clone.clone.1 | custom fusion | bytes 8388640 | tf_op jit(solution)/shard_map/while/body/eval_jaxpr/gather | solution.py:58
  69.1 4.7 %fusion.66 = (bf16[1024,1024]{1,0:T(8,128)(2,1)}, bf16[1024,1024]{1,0:T(8,128)(2,1)}) fusion(bf16[1024,2048]{1,0:T(8,128)(2,1)} %bitcast.74), kind=kLoop, calls=%fused_computation.66.clone.1 | loop fusion | bytes 8388608 | tf_op jit(solution)/shard_map/while/body/eval_jaxpr/slice | solution.py:59
  73.7 2.9 %copy.38 = bf16[1024,1024]{0,1:T(8,128)(2,1)S(1)} copy(bf16[1024,1024]{1,0:T(8,128)(2,1)} %get-tuple-element.136) | data formatting | bytes 4194304 | tf_op jit(solution)/shard_map/while
  76.6 0.2 reshape.183
  76.8 0.7 fusion.67
  77.5 0.6 dynamic_slice.44
  78.0 0.5 iota_compare_fusion.2
  78.6 0.0 copy-start.2
  78.6 3.3 %fusion.68 = (f32[16,64]{1,0:T(8,128)S(1)}, f32[16,64,1024]{2,1,0:T(8,128)}) fusion(f32[16,64,1024]{2,1,0:T(8,128)S(1)} %fusion.67, pred[1024]{0:T(1024)(128)(4,1)S(1)} %iota_compare_fusion.2), kind=kOutput, calls=%fused_computation.67.clone.1 | output fusion | flops 6292479 | bytes 8393728 | tf_op jit(solution)/shard_map/while/body/eval_jaxpr/sub | solution.py:32
  81.9 0.0 copy-done.2
  81.9 2.6 %copy.37 = bf16[1024,1024]{0,1:T(8,128)(2,1)} copy(bf16[1024,1024]{1,0:T(8,128)(2,1)S(1)} %copy-done.2) | data formatting | bytes 4194304 | tf_op jit(solution)/shard_map/while
  84.5 3.6 %fusion.69 = bf16[16,64,64]{2,1,0:T(8,128)(2,1)S(1)} fusion(bf16[1024,16,64]{0,2,1:T(8,128)(2,1)} %bitcast.76, f32[16,64,1024]{2,1,0:T(8,128)} %get-tuple-element.137, f32[16,64]{1,0:T(8,128)S(1)} %get-tuple-element.138), kind=kOutput, calls=%fused_computation.11.clone.1 | convolution fusion | flops 136380416 | bytes 6426624 | tf_op jit(solution)/shard_map/while/body/eval_jaxpr/hqk,khd->qhd/dot_general | solution.py:67
  88.1 0.1 copy.39
  88.3 6.8 %gather_fusion = bf16[8,128,2048]{2,1,0:T(8,128)(2,1)} fusion(bf16[20,128,2048]{2,1,0:T(8,128)(2,1)} %get-tuple-element.156, s32[1024]{0:T(1024)S(1)} %pad_clamp_fusion.2), kind=kCustom, calls=%fused_computation.clone.clone.1 | custom fusion | bytes 8388640 | tf_op jit(solution)/shard_map/while/body/eval_jaxpr/gather | solution.py:58
  95.1 4.7 %fusion.66 = (bf16[1024,1024]{1,0:T(8,128)(2,1)}, bf16[1024,1024]{1,0:T(8,128)(2,1)}) fusion(bf16[1024,2048]{1,0:T(8,128)(2,1)} %bitcast.74), kind=kLoop, calls=%fused_computation.66.clone.1 | loop fusion | bytes 8388608 | tf_op jit(solution)/shard_map/while/body/eval_jaxpr/slice | solution.py:59
  99.8 2.9 %copy.38 = bf16[1024,1024]{0,1:T(8,128)(2,1)S(1)} copy(bf16[1024,1024]{1,0:T(8,128)(2,1)} %get-tuple-element.136) | data formatting | bytes 4194304 | tf_op jit(solution)/shard_map/while
  102.7 0.2 reshape.183
  102.9 0.7 fusion.67
  103.5 0.6 dynamic_slice.44
  104.1 0.5 iota_compare_fusion.2
  104.7 3.3 %fusion.68 = (f32[16,64]{1,0:T(8,128)S(1)}, f32[16,64,1024]{2,1,0:T(8,128)}) fusion(f32[16,64,1024]{2,1,0:T(8,128)S(1)} %fusion.67, pred[1024]{0:T(1024)(128)(4,1)S(1)} %iota_compare_fusion.2), kind=kOutput, calls=%fused_computation.67.clone.1 | output fusion | flops 6292479 | bytes 8393728 | tf_op jit(solution)/shard_map/while/body/eval_jaxpr/sub | solution.py:32
  108.0 2.6 %copy.37 = bf16[1024,1024]{0,1:T(8,128)(2,1)} copy(bf16[1024,1024]{1,0:T(8,128)(2,1)S(1)} %copy-done.2) | data formatting | bytes 4194304 | tf_op jit(solution)/shard_map/while
  110.5 3.6 %fusion.69 = bf16[16,64,64]{2,1,0:T(8,128)(2,1)S(1)} fusion(bf16[1024,16,64]{0,2,1:T(8,128)(2,1)} %bitcast.76, f32[16,64,1024]{2,1,0:T(8,128)} %get-tuple-element.137, f32[16,64]{1,0:T(8,128)S(1)} %get-tuple-element.138), kind=kOutput, calls=%fused_computation.11.clone.1 | convolution fusion | flops 136380416 | bytes 6426624 | tf_op jit(solution)/shard_map/while/body/eval_jaxpr/hqk,khd->qhd/dot_general | solution.py:67
  114.1 0.1 copy.39
  114.3 2.0 fusion.23
  116.4 4.9 %collective-permute-start.2 = (bf16[128,1024]{1,0:T(8,128)(2,1)S(1)}, bf16[128,1024]{1,0:T(8,128)(2,1)S(1)}, u32[]{:S(2)}, u32[]{:S(2)}) collective-permute-start(bf16[128,1024]{1,0:T(8,128)(2,1)S(1)} %fusion.23), channel_id=1, source_target_pairs={{0,1},{1,2},{2,3},{3,0},{4,5},{5,6},{6,7},{7,4},{8,9},{9,10},{10,1... | collective-permute-start | bytes 786440 | tf_op jit(solution)/shard_map/ppermute | solution.py:85
  121.3 2.8 %collective-permute-done.2 = bf16[128,1024]{1,0:T(8,128)(2,1)S(1)} collective-permute-done((bf16[128,1024]{1,0:T(8,128)(2,1)S(1)}, bf16[128,1024]{1,0:T(8,128)(2,1)S(1)}, u32[]{:S(2)}, u32[]{:S(2)}) %collective-permute-start.2) | collective-permute-done | bytes 262176 | tf_op jit(solution)/shard_map/ppermute | solution.py:85
  124.1 3.0 %collective-permute-start.3 = (bf16[128,1024]{1,0:T(8,128)(2,1)S(1)}, bf16[128,1024]{1,0:T(8,128)(2,1)S(1)}, u32[]{:S(2)}, u32[]{:S(2)}) collective-permute-start(bf16[128,1024]{1,0:T(8,128)(2,1)S(1)} %collective-permute-done.2), channel_id=1, source_target_pairs={{0,1},{1,2},{2,3},{3,0},{4,5},{5,6},{6,7},{7,4},{8,9},{9,10},{10,1... | collective-permute-start | bytes 786440 | tf_op jit(solution)/shard_map/ppermute | solution.py:85
  127.1 2.8 %collective-permute-done.3 = bf16[128,1024]{1,0:T(8,128)(2,1)S(1)} collective-permute-done((bf16[128,1024]{1,0:T(8,128)(2,1)S(1)}, bf16[128,1024]{1,0:T(8,128)(2,1)S(1)}, u32[]{:S(2)}, u32[]{:S(2)}) %collective-permute-start.3) | collective-permute-done | bytes 262176 | tf_op jit(solution)/shard_map/ppermute | solution.py:85
  129.9 3.0 %collective-permute-start.4 = (bf16[128,1024]{1,0:T(8,128)(2,1)S(1)}, bf16[128,1024]{1,0:T(8,128)(2,1)S(1)}, u32[]{:S(2)}, u32[]{:S(2)}) collective-permute-start(bf16[128,1024]{1,0:T(8,128)(2,1)S(1)} %collective-permute-done.3), channel_id=1, source_target_pairs={{0,1},{1,2},{2,3},{3,0},{4,5},{5,6},{6,7},{7,4},{8,9},{9,10},{10,1... | collective-permute-start | bytes 786440 | tf_op jit(solution)/shard_map/ppermute | solution.py:85
  132.9 0.0 all-gather.2.cloned.1.call-update
  133.0 2.7 %collective-permute-done.4 = bf16[128,1024]{1,0:T(8,128)(2,1)S(1)} collective-permute-done((bf16[128,1024]{1,0:T(8,128)(2,1)S(1)}, bf16[128,1024]{1,0:T(8,128)(2,1)S(1)}, u32[]{:S(2)}, u32[]{:S(2)}) %collective-permute-start.4) | collective-permute-done | bytes 262176 | tf_op jit(solution)/shard_map/ppermute | solution.py:85
  135.9 2.5 %convolution_convert_fusion.1 = bf16[512,3,256]{0,2,1:T(8,128)(2,1)S(1)} fusion(bf16[3,1024,256]{2,1,0:T(8,128)(2,1)} %param.16, bf16[1024,1024]{1,0:T(8,128)(2,1)S(1)} %constant_dynamic-update-slice_fusion.1, s32[]{:T(128)S(6)} %select_n.37), kind=kOutput, calls=%fused_computation.38 | convolution fusion | flops 805699584 | bytes 3407876 | tf_op jit(solution)/shard_map/rd,tdc->rtc/dot_general | solution.py:89
  138.4 5.5 %collective-permute-start.5 = (bf16[512,512]{0,1:T(8,128)(2,1)S(1)}, bf16[512,512]{0,1:T(8,128)(2,1)S(1)}, u32[]{:S(2)}, u32[]{:S(2)}) collective-permute-start(bf16[512,512]{0,1:T(8,128)(2,1)S(1)} %slice.49), channel_id=1, source_target_pairs={{0,4},{4,8},{8,12},{12,16},{16,20},{20,24},{24,28},{1,5},{5,9},{9,... | collective-permute-start | bytes 1572872 | tf_op jit(solution)/shard_map/ppermute | solution.py:23
  143.8 2.1 %collective-permute-start.6 = (bf16[512,512]{0,1:T(8,128)(2,1)S(1)}, bf16[512,512]{0,1:T(8,128)(2,1)S(1)}, u32[]{:S(2)}, u32[]{:S(2)}) collective-permute-start(bf16[512,512]{0,1:T(8,128)(2,1)S(1)} %slice.49), channel_id=1, source_target_pairs={{4,0},{8,4},{12,8},{16,12},{20,16},{24,20},{28,24},{5,1},{9,5},{13... | collective-permute-start | bytes 1572872 | tf_op jit(solution)/shard_map/ppermute | solution.py:24
  146.0 1.0 fusion.21
  147.0 19.2 %collective-permute-done.5 = bf16[512,512]{0,1:T(8,128)(2,1)S(1)} collective-permute-done((bf16[512,512]{0,1:T(8,128)(2,1)S(1)}, bf16[512,512]{0,1:T(8,128)(2,1)S(1)}, u32[]{:S(2)}, u32[]{:S(2)}) %collective-permute-start.5) | collective-permute-done | bytes 524320 | tf_op jit(solution)/shard_map/ppermute | solution.py:23
  166.2 1.5 collective-permute-done.6
  167.7 0.1 pad_maximum_fusion.1
  167.8 1.3 fusion.36
  169.1 9.8 %fusion.37 = (f32[4,512]{1,0:T(4,128)S(1)}, f32[4,512,1536]{2,1,0:T(8,128)}) fusion(pred[512,1536]{1,0:T(8,128)(4,1)S(1)} %fusion.21, bf16[512,4,64]{0,2,1:T(8,128)(2,1)S(1)} %bitcast.87, bf16[1536,4,64]{0,2,1:T(8,128)(2,1)} %bitcast.86), kind=kOutput, calls=%fused_computation.70 | convolution fusion | flops 415237632 | bytes 14426112 | tf_op jit(solution)/shard_map/while/body/eval_jaxpr/sub | solution.py:32
  178.9 7.0 %fusion.25 = bf16[512,4,64]{0,2,1:T(8,128)(2,1)S(1)} fusion(bf16[1536,4,64]{0,2,1:T(8,128)(2,1)} %bitcast.85, f32[4,512,1536]{2,1,0:T(8,128)} %get-tuple-element.93, f32[4,512]{1,0:T(4,128)S(1)} %get-tuple-element.92), kind=kOutput, calls=%fused_computation.45 | convolution fusion | flops 409075712 | bytes 13639680 | tf_op jit(solution)/shard_map/while/body/eval_jaxpr/hqk,khd->qhd/dot_general | solution.py:117
  186.0 0.1 convert_element_type.65
  186.1 8.4 %all_to_all.16 = bf16[4,128,256]{1,2,0:T(8,128)(2,1)S(1)} all-to-all(bf16[4,128,256]{1,2,0:T(8,128)(2,1)S(1)} %copy.18), channel_id=1, replica_groups=mesh['band'=8,'head'=4] {'head'}, dimensions={0} | all-to-all | bytes 524288 | tf_op jit(solution)/shard_map/all_to_all | solution.py:125
  194.5 2.8 %fusion.24 = bf16[128,1024]{1,0:T(8,128)(2,1)} fusion(bf16[128,1024]{0,1:T(8,128)(2,1)S(1)} %bitcast.82, bf16[1024,1024]{1,0:T(8,128)(2,1)} %all-gather.2.cloned.1.call-done, bf16[128,1024]{1,0:T(8,128)(2,1)S(1)} %fusion.23), kind=kOutput, calls=%fused_computation.44 | convolution fusion | flops 268828672 | bytes 2883584 | tf_op jit(solution)/shard_map/dot_general | solution.py:127
  (34 shorter events, 0.4 us)
Async XLA Ops:
  6.5 27.2 %copy-start = (bf16[1024,1024]{1,0:T(8,128)(2,1)S(1)}, bf16[1024,1024]{1,0:T(8,128)(2,1)}, u32[]{:S(2)}) copy-start(bf16[1024,1024]{1,0:T(8,128)(2,1)} %param.13) | copy-start | bytes 6291460
  6.5 188.0 %all-gather.2.cloned.1.call-start = ((), (), s32[]{:S(2)}) async-start(), calls=%async_computation.1 | async-start | bytes 2621440 | tf_op jit(solution)/shard_map/all_gather | solution.py:126
  18.6 3.3 %copy-start.3 = (bf16[2048,2048]{1,0:T(8,128)(2,1)}, bf16[2048,2048]{1,0:T(8,128)(2,1)S(1)}, u32[]{:S(2)}) copy-start(bf16[2048,2048]{1,0:T(8,128)(2,1)S(1)} %convolution_convert_fusion) | copy-start | bytes 25165828
  23.1 10.6 %copy-start.5 = (s32[2,8]{1,0:T(2,128)S(1)}, s32[2,8]{1,0:T(2,128)}, u32[]{:S(2)}) copy-start(s32[2,8]{1,0:T(2,128)} %param.18) | copy-start | bytes 196
  23.1 10.6 %copy-start.4 = (bf16[128,1024]{1,0:T(8,128)(2,1)S(1)}, bf16[128,1024]{1,0:T(8,128)(2,1)}, u32[]{:S(2)}) copy-start(bf16[128,1024]{1,0:T(8,128)(2,1)} %param.12) | copy-start | bytes 786436
  26.2 16.3 %collective-permute-start.1 = (bf16[2,262144]{1,0:T(2,128)(2,1)}, bf16[2,262144]{1,0:T(2,128)(2,1)}, u32[]{:S(2)}, u32[]{:S(2)}) collective-permute-start(bf16[2,262144]{1,0:T(2,128)(2,1)} %slice.36), channel_id=1, source_target_pairs={{1,0},{2,1},{3,2},{4,3},{5,4},{6,5},{7,6},{8,7},{9,8},{10,9},{11,1... | collective-permute-start | bytes 3145736 | tf_op jit(solution)/shard_map/ppermute | solution.py:24
  31.6 18.3 %collective-permute-start = (bf16[2,262144]{1,0:T(2,128)(2,1)}, bf16[2,262144]{1,0:T(2,128)(2,1)}, u32[]{:S(2)}, u32[]{:S(2)}) collective-permute-start(bf16[2,262144]{1,0:T(2,128)(2,1)} %slice.34), channel_id=1, source_target_pairs={{0,1},{1,2},{2,3},{3,4},{4,5},{5,6},{6,7},{7,8},{8,9},{9,10},{10,1... | collective-permute-start | bytes 3145736 | tf_op jit(solution)/shard_map/ppermute | solution.py:23
  51.5 10.7 %copy-start.6 = (s32[2]{0:T(128)S(1)}, s32[2]{0:T(128)}, u32[]{:S(2)}) copy-start(s32[2]{0:T(128)} %param.19) | copy-start | bytes 28
  78.6 3.3 %copy-start.2 = (bf16[1024,1024]{1,0:T(8,128)(2,1)S(1)}, bf16[1024,1024]{1,0:T(8,128)(2,1)}, u32[]{:S(2)}) copy-start(bf16[1024,1024]{1,0:T(8,128)(2,1)} %get-tuple-element.135) | copy-start | bytes 6291460 | tf_op jit(solution)/shard_map/while
  104.7 3.3 %copy-start.2 = (bf16[1024,1024]{1,0:T(8,128)(2,1)S(1)}, bf16[1024,1024]{1,0:T(8,128)(2,1)}, u32[]{:S(2)}) copy-start(bf16[1024,1024]{1,0:T(8,128)(2,1)} %get-tuple-element.135) | copy-start | bytes 6291460 | tf_op jit(solution)/shard_map/while
  116.4 7.7 %collective-permute-start.2 = (bf16[128,1024]{1,0:T(8,128)(2,1)S(1)}, bf16[128,1024]{1,0:T(8,128)(2,1)S(1)}, u32[]{:S(2)}, u32[]{:S(2)}) collective-permute-start(bf16[128,1024]{1,0:T(8,128)(2,1)S(1)} %fusion.23), channel_id=1, source_target_pairs={{0,1},{1,2},{2,3},{3,0},{4,5},{5,6},{6,7},{7,4},{8,9},{9,10},{10,1... | collective-permute-start | bytes 786440 | tf_op jit(solution)/shard_map/ppermute | solution.py:85
  124.1 5.8 %collective-permute-start.3 = (bf16[128,1024]{1,0:T(8,128)(2,1)S(1)}, bf16[128,1024]{1,0:T(8,128)(2,1)S(1)}, u32[]{:S(2)}, u32[]{:S(2)}) collective-permute-start(bf16[128,1024]{1,0:T(8,128)(2,1)S(1)} %collective-permute-done.2), channel_id=1, source_target_pairs={{0,1},{1,2},{2,3},{3,0},{4,5},{5,6},{6,7},{7,4},{8,9},{9,10},{10,1... | collective-permute-start | bytes 786440 | tf_op jit(solution)/shard_map/ppermute | solution.py:85
  129.9 5.8 %collective-permute-start.4 = (bf16[128,1024]{1,0:T(8,128)(2,1)S(1)}, bf16[128,1024]{1,0:T(8,128)(2,1)S(1)}, u32[]{:S(2)}, u32[]{:S(2)}) collective-permute-start(bf16[128,1024]{1,0:T(8,128)(2,1)S(1)} %collective-permute-done.3), channel_id=1, source_target_pairs={{0,1},{1,2},{2,3},{3,0},{4,5},{5,6},{6,7},{7,4},{8,9},{9,10},{10,1... | collective-permute-start | bytes 786440 | tf_op jit(solution)/shard_map/ppermute | solution.py:85
  138.4 27.9 %collective-permute-start.5 = (bf16[512,512]{0,1:T(8,128)(2,1)S(1)}, bf16[512,512]{0,1:T(8,128)(2,1)S(1)}, u32[]{:S(2)}, u32[]{:S(2)}) collective-permute-start(bf16[512,512]{0,1:T(8,128)(2,1)S(1)} %slice.49), channel_id=1, source_target_pairs={{0,4},{4,8},{8,12},{12,16},{16,20},{20,24},{24,28},{1,5},{5,9},{9,... | collective-permute-start | bytes 1572872 | tf_op jit(solution)/shard_map/ppermute | solution.py:23
  143.8 23.9 %collective-permute-start.6 = (bf16[512,512]{0,1:T(8,128)(2,1)S(1)}, bf16[512,512]{0,1:T(8,128)(2,1)S(1)}, u32[]{:S(2)}, u32[]{:S(2)}) collective-permute-start(bf16[512,512]{0,1:T(8,128)(2,1)S(1)} %slice.49), channel_id=1, source_target_pairs={{4,0},{8,4},{12,8},{16,12},{20,16},{24,20},{28,24},{5,1},{9,5},{13... | collective-permute-start | bytes 1572872 | tf_op jit(solution)/shard_map/ppermute | solution.py:24
  178.9 18.3 %copy-start.1 = (bf16[1024,1024]{1,0:T(8,128)(2,1)S(1)}, bf16[1024,1024]{1,0:T(8,128)(2,1)}, u32[]{:S(2)}) copy-start(bf16[1024,1024]{1,0:T(8,128)(2,1)} %param.13) | copy-start | bytes 6291460
Sparse Core Ops, SparseCore 0:
  133.0 23.1 all-gather.1
